TPU v7x, 512 devices: a whole 4x8x8 slice. The times are simulated.
512 devices in a mesh: dp: 32 (over x, y), table: 16 (over z, core).
Axes of the slice: x: 4, y: 8, z: 8, core: 2. Of those that a mesh axis runs over, the one named last changes fastest.
Arguments:
- table: bfloat16 [12288, 512], P('table'), may hold values from -6 to 6
- history_shard: int32 [512, 256, 1], P(('dp', 'table')), may hold values from 0 to 15; in each aligned block of 256 rows (0 to 255, 256 to 511, ..., all dimensions but the last counted through in order) at most 32 rows name the same one
- history_row: int32 [512, 256], P(('dp', 'table')), may hold values from 0 to 767
- lengths: int32 [512], P(('dp', 'table')), may hold values from 1 to 256, 98304 in all
- w_in: bfloat16 [512, 2048], replicated, may hold values from -0.25 to 0.25
- w_out: bfloat16 [512, 512], replicated, may hold values from -0.25 to 0.25
- cotangent: bfloat16 [512, 256, 512], P(('dp', 'table')), may hold values from -6 to 6
Outputs:
- table_grad: float32 [12288, 512], P('table')
- dense_grad: bfloat16 [512, 512], replicated
Inputs may be any that keep to these rules, and one draw needn't show every extreme that they name: `history_shard`: among the 256 history slots of one device's samples, at most 32 name one table shard, and that bound is met by some shard in some device's slots. `lengths`: some sample has the full length 256.
All inputs are finite; a program needn't handle non-finite values. No bound on the sum of `lengths` on one device may be relied on, other than what follows from the above.
Results may differ from a plain program's by a relative error of at most 0.017.
Values may be sent and summed in bfloat16 or wider, within the bound.
A program may use at most 64 MiB of HBM per device.

v0:
```python
import math
import jax
import jax.numpy as jnp
from jax import lax
from jax.sharding import PartitionSpec as P

HEADS = 4


def layer_norm(values):
    average = jnp.mean(values, axis=-1, keepdims=True)
    centred = values - average
    variance = jnp.mean(centred * centred, axis=-1, keepdims=True)
    return centred * lax.rsqrt(variance + 1e-06)


def hstu_layer(embedded, w_in, w_out, lengths):
    samples_here, seq_span, model_width = embedded.shape
    head_dim = model_width // HEADS
    normed = layer_norm(embedded.astype(jnp.float32)).astype(jnp.bfloat16)
    projected = jax.nn.silu(
        jnp.dot(
            normed.reshape(samples_here * seq_span, model_width),
            w_in,
            preferred_element_type=jnp.float32,
        )
    )
    gate_part = projected[:, :model_width]
    shaped = (samples_here, seq_span, HEADS, head_dim)
    values = projected[:, model_width : 2 * model_width].astype(jnp.bfloat16).reshape(shaped)
    queries = projected[:, 2 * model_width : 3 * model_width].astype(jnp.bfloat16).reshape(shaped)
    keys = projected[:, 3 * model_width :].astype(jnp.bfloat16).reshape(shaped)
    scores = jnp.einsum(
        "blhd,bmhd->bhlm", queries.astype(jnp.float32), keys.astype(jnp.float32)
    ) * head_dim ** (-0.5)
    positions = jnp.arange(seq_span)
    live_keys = (positions[None, None, :] <= positions[None, :, None]) & (
        positions[None, None, :] < lengths[:, None, None]
    )
    weights = (
        jnp.where(live_keys[:, None], jax.nn.silu(scores), 0.0)
        / lengths.astype(jnp.float32)[:, None, None, None]
    )
    weights = weights.astype(jnp.bfloat16)
    attended = jnp.einsum(
        "bhlm,bmhd->blhd", weights.astype(jnp.float32), values.astype(jnp.float32)
    ).reshape(samples_here * seq_span, model_width)
    mixed = (layer_norm(attended) * gate_part).astype(jnp.bfloat16)
    output = jnp.dot(mixed, w_out, preferred_element_type=jnp.float32) + embedded.reshape(
        -1, model_width
    ).astype(jnp.float32)
    return (output, mixed)


def per_device(table, history_shard, history_row, lengths, w_in, w_out, cotangent):
    shard_rows, model_width = table.shape
    samples_here, seq_span = history_row.shape
    groups = lax.axis_size("table")
    slot_count = samples_here * seq_span
    capacity = 2 * slot_count // groups
    owners = history_shard[:, :, 0].reshape(-1)
    local_rows = history_row.reshape(-1)
    owner_hits = (owners[:, None] == jnp.arange(groups)[None, :]).astype(jnp.int32)
    slot_rank = jnp.sum((jnp.cumsum(owner_hits, axis=0) - owner_hits) * owner_hits, axis=1)
    position = owners * capacity + slot_rank
    requested = (
        jnp.zeros((groups * capacity,), jnp.int32)
        .at[position]
        .set(local_rows)
        .reshape(groups, capacity)
    )
    incoming = lax.all_to_all(requested, "table", split_axis=0, concat_axis=0, tiled=True).reshape(
        -1
    )
    global_rows = owners * shard_rows + local_rows
    piece = lax.all_gather(table, "table", axis=0, tiled=True)
    inside = (global_rows >= 0) & (global_rows < piece.shape[0])
    taken = piece[jnp.clip(global_rows, 0, piece.shape[0] - 1)].astype(jnp.float32)
    embedded = jnp.where(inside[:, None], taken, 0.0).astype(jnp.bfloat16)
    embedded = embedded.reshape(samples_here, seq_span, model_width)
    output, pullback, mixed = jax.vjp(
        lambda rows_in: hstu_layer(rows_in, w_in, w_out, lengths), embedded, has_aux=True
    )
    row_live = jnp.arange(seq_span)[None, :] < lengths[:, None]
    grad_seed = jnp.where(row_live[:, :, None], cotangent, jnp.zeros_like(cotangent))
    flat_seed = grad_seed.reshape(-1, model_width)
    (row_grad,) = pullback(flat_seed.astype(jnp.float32))
    dense_part = jnp.dot(mixed.T, flat_seed, preferred_element_type=jnp.float32)
    outgoing = (
        jnp.zeros((groups * capacity, model_width), jnp.bfloat16)
        .at[position]
        .set(row_grad.reshape(-1, model_width))
    )
    arrived = lax.all_to_all(
        outgoing.reshape(groups, capacity, model_width),
        "table",
        split_axis=0,
        concat_axis=0,
        tiled=True,
    )
    local_grad = (
        jnp.zeros((shard_rows, model_width), jnp.float32)
        .at[incoming]
        .add(arrived.reshape(-1, model_width).astype(jnp.float32))
    )
    total_slots = slot_count * lax.axis_size("dp") * groups
    grad_scale = 1.0 / math.sqrt(total_slots)
    table_grad = lax.psum(local_grad, "dp")
    dense_total = lax.psum(dense_part, ("dp", "table"))
    dense_grad = (dense_total * grad_scale).astype(jnp.bfloat16)
    return (table_grad, dense_grad)


def solution(mesh):
    in_specs = (
        P("table", None),
        P(("dp", "table"), None, None),
        P(("dp", "table"), None),
        P(("dp", "table")),
        P(),
        P(),
        P(("dp", "table"), None, None),
    )
    out_specs = (P("table", None), P())
    return jax.shard_map(
        per_device, mesh=mesh, in_specs=in_specs, out_specs=out_specs, check_vma=False
    )
```

profile of v0, /device:TPU:64, one launch (start us, length us, event | category | flops | bytes accessed | tf_op | source)
XLA Modules:
  0.0 582.9 jit_solution(10138484838293075610)
XLA Ops:
  10.9 1.6 scatter_custom_fusion
  13.1 10.0 %all-to-all-start = ((s32[16,1,32]{2,1,0:T(1,128)}), s32[16,1,32]{2,1,0:T(1,128)S(1)}, u32[]{:S(2)}, u32[]{:S(2)}) async-start(s32[16,1,32]{2,1,0:T(1,128)} %all_to_all.9), calls=%async_computation | async-start | bytes 16384 | tf_op jit(solution)/shard_map/all_to_all | solution.py:72
  24.5 66.3 %all-gather.2.cloned.1.call-done = bf16[12288,512]{1,0:T(8,128)(2,1)} async-done(((bf16[768,512]{1,0:T(8,128)(2,1)}), bf16[12288,512]{1,0:T(8,128)(2,1)}) %all-gather.2.cloned.1.call-update) | async-done | bytes 12582928 | tf_op jit(solution)/shard_map/all_gather | solution.py:76
  90.8 7.4 %gather_fusion = bf16[256,512]{1,0:T(8,128)(2,1)S(1)} fusion(bf16[12288,512]{1,0:T(8,128)(2,1)} %all-gather.2.cloned.1.call-done, s32[1024]{0:T(1024)S(1)} %pad_clamp_fusion), kind=kCustom, calls=%fused_computation | custom fusion | bytes 525312 | tf_op jit(solution)/shard_map/gather | solution.py:78
  98.7 2.8 fusion.76
  102.5 1.6 divide_convert_fusion
  105.1 1.7 multiply_reduce_fusion.1
  106.9 2.1 fusion.75
  109.2 2.0 fusion.26
  111.5 1.0 fusion.79
  112.5 0.9 fusion.81
  113.6 1.8 copy.38
  115.4 1.8 copy.39
  117.2 3.4 multiply_reduce_fusion
  120.6 1.0 fusion.74
  121.6 2.9 scatter_custom_fusion.1
  124.5 6.9 %all-to-all-start.1 = ((bf16[16,32,512]{2,1,0:T(8,128)(2,1)}), bf16[16,32,512]{2,1,0:T(8,128)(2,1)}, u32[]{:S(2)}, u32[]{:S(2)}) async-start(bf16[16,32,512]{2,1,0:T(8,128)(2,1)} %bitcast.120), calls=%async_computation.1 | async-start | bytes 1048576 | tf_op jit(solution)/shard_map/all_to_all | solution.py:94
  131.6 2.5 fusion.45
  135.4 10.4 %all-to-all-done.1 = bf16[16,32,512]{2,1,0:T(8,128)(2,1)} async-done(((bf16[16,32,512]{2,1,0:T(8,128)(2,1)}), bf16[16,32,512]{2,1,0:T(8,128)(2,1)}, u32[]{:S(2)}, u32[]{:S(2)}) %all-to-all-start.1) | async-done | bytes 524320 | tf_op jit(solution)/shard_map/all_to_all | solution.py:94
  145.8 5.5 scatter_custom_fusion.2
  151.3 258.6 %all-reduce.9.cloned.1.call-done = f32[512,512]{1,0:T(8,128)} async-done(((f32[512,512]{1,0:T(8,128)}), f32[512,512]{1,0:T(8,128)}) %all-reduce.9.cloned.1.call-update) | async-done | bytes 1048592 | tf_op jit(solution)/shard_map/psum | solution.py:109
  409.9 2.1 multiply_convert_fusion
  412.0 161.6 %all-reduce.7.cloned.1.call-done = f32[768,512]{1,0:T(8,128)} async-done(((f32[768,512]{1,0:T(8,128)}), f32[768,512]{1,0:T(8,128)}) %all-reduce.7.cloned.1.call-update) | async-done | bytes 1572880 | tf_op jit(solution)/shard_map/psum | solution.py:108
  573.7 2.7 copy.58
  (60 shorter events, 9.8 us)
Async XLA Ops:
  7.2 91.5 %copy-start = (bf16[512,2048]{1,0:T(8,128)(2,1)S(1)}, bf16[512,2048]{1,0:T(8,128)(2,1)}, u32[]{:S(2)}) copy-start(bf16[512,2048]{1,0:T(8,128)(2,1)} %param.11) | copy-start | bytes 6291460
  7.2 83.6 %all-gather.2.cloned.1.call-start = ((), (), s32[]{:S(2)}) async-start(), calls=%async_computation.2 | async-start | bytes 13369344 | tf_op jit(solution)/shard_map/all_gather | solution.py:76
  13.1 111.4 %all-to-all-start = ((s32[16,1,32]{2,1,0:T(1,128)}), s32[16,1,32]{2,1,0:T(1,128)S(1)}, u32[]{:S(2)}, u32[]{:S(2)}) async-start(s32[16,1,32]{2,1,0:T(1,128)} %all_to_all.9), calls=%async_computation | async-start | bytes 16384 | tf_op jit(solution)/shard_map/all_to_all | solution.py:72
  102.4 1.8 copy-start.4
  102.5 1.6 copy-start.6
  102.5 1.6 copy-start.8
  104.1 0.8 copy-start.2
  109.2 2.1 copy-start.5
  109.2 2.3 copy-start.7
  111.2 1.3 copy-start.3
  117.2 4.4 copy-start.1
  124.5 21.3 %all-to-all-start.1 = ((bf16[16,32,512]{2,1,0:T(8,128)(2,1)}), bf16[16,32,512]{2,1,0:T(8,128)(2,1)}, u32[]{:S(2)}, u32[]{:S(2)}) async-start(bf16[16,32,512]{2,1,0:T(8,128)(2,1)} %bitcast.120), calls=%async_computation.1 | async-start | bytes 1048576 | tf_op jit(solution)/shard_map/all_to_all | solution.py:94
  131.4 278.5 %all-reduce.9.cloned.1.call-start = ((), (), s32[]{:S(2)}) async-start(), calls=%async_computation.4 | async-start | bytes 2097152 | tf_op jit(solution)/shard_map/psum | solution.py:109
  134.1 439.6 %all-reduce.7.cloned.1.call-start = ((), (), s32[]{:S(2)}) async-start(), calls=%async_computation.3 | async-start | bytes 3145728 | tf_op jit(solution)/shard_map/psum | solution.py:108
Sparse Core Ops, SparseCore 0:
  10.1 80.5 all-gather.1
  137.3 272.5 all-reduce.8
  414.3 159.3 all-reduce.6
where the time goes:
time: 584 us; the launch traced here: 583 us
  waiting for transfers between devices  498 us (85%)
  local copies, waits for them, and re-layouts  18.5 us (3%)
  other arithmetic  18.5 us (3%)
  starting transfers between devices  17.1 us (3%)
  matrix products  16.5 us (3%)
  between operations  14.6 us (2%)
    psum x1, waiting for transfers between devices, per_device(): dense_total = lax.psum(dense_part, ('dp', 'table'))  259 us
    psum x1, waiting for transfers between devices, per_device(): table_grad = lax.psum(local_grad, 'dp')  162 us
    all_gather x1, waiting for transfers between devices, per_device(): piece = lax.all_gather(table, 'table', axis=0, tiled=True)  66.3 us
  transfers between devices with their start and end apart: 5, of which 4 were waited for; matrix products, arithmetic and copies ran while one was open for 9% of the time, Pallas kernels for 0%

commit v1 on v0

--- a/solution.py
+++ b/solution.py
@@ -106,7 +106,9 @@
     total_slots = slot_count * lax.axis_size("dp") * groups
     grad_scale = 1.0 / math.sqrt(total_slots)
     table_grad = lax.psum(local_grad, "dp")
-    dense_total = lax.psum(dense_part, ("dp", "table"))
+    dense_total = dense_part
+    for mesh_axis in ("table", "dp"):
+        dense_total = lax.psum(dense_total, mesh_axis)
     dense_grad = (dense_total * grad_scale).astype(jnp.bfloat16)
     return (table_grad, dense_grad)
 

time: 584 us -> 435 us (0.74)
  the two profiles are of different devices: /device:TPU:64 before, /device:TPU:2 now
where the time goes in v1:
time: 435 us; the launch traced here: 434 us
  waiting for transfers between devices  352 us (81%)
  other arithmetic  18.5 us (4%)
  local copies, waits for them, and re-layouts  17 us (4%)
  matrix products  16.5 us (4%)
  starting transfers between devices  15 us (3%)
  between operations  14.6 us (3%)
    psum x1, waiting for transfers between devices, per_device(): table_grad = lax.psum(local_grad, 'dp')  170 us
    psum x1, waiting for transfers between devices, per_device(): dense_total = lax.psum(dense_total, mesh_axis)  100 us
    all_gather x1, waiting for transfers between devices, per_device(): piece = lax.all_gather(table, 'table', axis=0, tiled=True)  68.9 us
    all_to_all x1, waiting for transfers between devices, per_device(): lax.all_to_all(outgoing.reshape(groups, capacity, model_width), 'table',...  12 us
    all_to_all x1, starting transfers between devices, per_device(): lax.all_to_all(requested, 'table', split_axis=0, concat_axis=0, tiled=True)  10.4 us
  transfers between devices with their start and end apart: 5, of which 4 were waited for; matrix products, arithmetic and copies ran while one was open for 11% of the time, Pallas kernels for 0%

profile of v1, /device:TPU:2, one launch (start us, length us, event | category | flops | bytes accessed | tf_op | source)
XLA Modules:
  0.0 434.1 jit_solution(14185518587502341418)
XLA Ops:
  10.9 1.6 scatter_custom_fusion
  13.1 10.4 %all-to-all-start = ((s32[16,1,32]{2,1,0:T(1,128)}), s32[16,1,32]{2,1,0:T(1,128)S(1)}, u32[]{:S(2)}, u32[]{:S(2)}) async-start(s32[16,1,32]{2,1,0:T(1,128)} %all_to_all.9), calls=%async_computation | async-start | bytes 16384 | tf_op jit(solution)/shard_map/all_to_all | solution.py:72
  25.0 68.9 %all-gather.2.cloned.1.call-done = bf16[12288,512]{1,0:T(8,128)(2,1)} async-done(((bf16[768,512]{1,0:T(8,128)(2,1)}), bf16[12288,512]{1,0:T(8,128)(2,1)}) %all-gather.2.cloned.1.call-update) | async-done | bytes 12582928 | tf_op jit(solution)/shard_map/all_gather | solution.py:76
  93.9 7.4 %gather_fusion = bf16[256,512]{1,0:T(8,128)(2,1)S(1)} fusion(bf16[12288,512]{1,0:T(8,128)(2,1)} %all-gather.2.cloned.1.call-done, s32[1024]{0:T(1024)S(1)} %pad_clamp_fusion), kind=kCustom, calls=%fused_computation | custom fusion | bytes 525312 | tf_op jit(solution)/shard_map/gather | solution.py:78
  101.8 2.8 fusion.76
  105.7 1.6 divide_convert_fusion
  108.3 1.7 multiply_reduce_fusion.1
  110.0 2.1 fusion.75
  112.3 2.0 fusion.26
  114.6 1.0 fusion.79
  115.6 0.9 fusion.81
  116.7 1.8 copy.38
  118.5 1.8 copy.39
  120.3 3.4 multiply_reduce_fusion
  123.7 1.0 fusion.74
  124.7 2.9 scatter_custom_fusion.1
  127.6 4.2 all-to-all-start.1
  132.1 2.5 fusion.45
  136.0 12.0 %all-to-all-done.1 = bf16[16,32,512]{2,1,0:T(8,128)(2,1)} async-done(((bf16[16,32,512]{2,1,0:T(8,128)(2,1)}), bf16[16,32,512]{2,1,0:T(8,128)(2,1)}, u32[]{:S(2)}, u32[]{:S(2)}) %all-to-all-start.1) | async-done | bytes 524320 | tf_op jit(solution)/shard_map/all_to_all | solution.py:94
  147.9 5.4 %scatter_custom_fusion.2 = f32[768,512]{1,0:T(8,128)} fusion(s32[512]{0:T(512)S(1)} %bitcast.137, bf16[512,512]{1,0:T(8,128)(2,1)} %bitcast.42, f32[]{:T(128)} %constant.15.clone.1), kind=kCustom, calls=%fused_computation.35 | custom fusion | flops 524288 | bytes 2097156 | tf_op jit(solution)/shard_map/scatter-add | solution.py:104
  153.3 100.4 %all-reduce.8.cloned.1.call-done = f32[512,512]{1,0:T(8,128)} async-done(((f32[512,512]{1,0:T(8,128)}), f32[512,512]{1,0:T(8,128)}) %all-reduce.8.cloned.1.call-update) | async-done | bytes 1048592 | tf_op jit(solution)/shard_map/psum | solution.py:111
  253.7 170.5 %all-reduce.10.cloned.1.call-done = (f32[768,512]{1,0:T(8,128)}, f32[512,512]{1,0:T(8,128)}) async-done(((f32[768,512]{1,0:T(8,128)}, f32[512,512]{1,0:T(8,128)}), (f32[768,512]{1,0:T(8,128)}, f32[512,512]{1,0:T(8,128)})) %all-reduce.10.cloned.1.call-update) | async-done | bytes 2621456 | tf_op jit(solution)/shard_map/psum | solution.py:108
  424.2 2.3 multiply_convert_fusion
  426.4 1.1 copy.59
  (62 shorter events, 9.8 us)
Async XLA Ops:
  7.2 94.6 %copy-start = (bf16[512,2048]{1,0:T(8,128)(2,1)S(1)}, bf16[512,2048]{1,0:T(8,128)(2,1)}, u32[]{:S(2)}) copy-start(bf16[512,2048]{1,0:T(8,128)(2,1)} %param.11) | copy-start | bytes 6291460
  7.2 86.7 %all-gather.2.cloned.1.call-start = ((), (), s32[]{:S(2)}) async-start(), calls=%async_computation.2 | async-start | bytes 13369344 | tf_op jit(solution)/shard_map/all_gather | solution.py:76
  13.1 114.5 %all-to-all-start = ((s32[16,1,32]{2,1,0:T(1,128)}), s32[16,1,32]{2,1,0:T(1,128)S(1)}, u32[]{:S(2)}, u32[]{:S(2)}) async-start(s32[16,1,32]{2,1,0:T(1,128)} %all_to_all.9), calls=%async_computation | async-start | bytes 16384 | tf_op jit(solution)/shard_map/all_to_all | solution.py:72
  105.5 1.7 copy-start.5
  105.7 1.6 copy-start.7
  105.7 1.6 copy-start.9
  107.3 0.8 copy-start.2
  112.3 2.1 copy-start.6
  112.3 2.3 copy-start.8
  114.4 1.3 copy-start.3
  120.3 4.4 %copy-start.1 = (bf16[1,256,512]{2,1,0:T(8,128)(2,1)S(1)}, bf16[1,256,512]{2,1,0:T(8,128)(2,1)}, u32[]{:S(2)}) copy-start(bf16[1,256,512]{2,1,0:T(8,128)(2,1)} %param.13) | copy-start | bytes 786436
  127.6 20.3 %all-to-all-start.1 = ((bf16[16,32,512]{2,1,0:T(8,128)(2,1)}), bf16[16,32,512]{2,1,0:T(8,128)(2,1)}, u32[]{:S(2)}, u32[]{:S(2)}) async-start(bf16[16,32,512]{2,1,0:T(8,128)(2,1)} %bitcast.120), calls=%async_computation.1 | async-start | bytes 1048576 | tf_op jit(solution)/shard_map/all_to_all | solution.py:94
  131.9 121.8 %all-reduce.8.cloned.1.call-start = ((), (), s32[]{:S(2)}) async-start(), calls=%async_computation.3 | async-start | bytes 2097152 | tf_op jit(solution)/shard_map/psum | solution.py:111
  134.6 289.5 %all-reduce.10.cloned.1.call-start = ((), (), s32[]{:S(2)}) async-start(), calls=%async_computation.4 | async-start | bytes 5242880 | tf_op jit(solution)/shard_map/psum | solution.py:108
  424.2 2.3 copy-start.4
Sparse Core Ops, SparseCore 0:
  10.1 83.7 all-gather.1
  135.1 118.5 all-reduce.7
  258.4 165.7 all-reduce.9
